TPU v7x, 128 devices: a whole 4x4x4 slice. The times are simulated.
128 devices in a mesh: plane: 4 (over x_hi, core), ray: 32 (over z, y, x_lo).
Axes of the slice: x: 4 (x_hi: 2, x_lo: 2; x = x_hi * 2 + x_lo), y: 4, z: 4, core: 2. Of those that a mesh axis runs over, the one named last changes fastest.
Arguments:
- coarse_potential: float32 [2048, 512], P(('plane', 'ray')), may hold values from -72 to 72
- fine_tiles: bfloat16 [4, 32768, 256], P('plane', 'ray'), may hold values from -0.59765625 to 0.59765625
- tile_requests: int32 [128, 4, 32, 16], P(('plane', 'ray')), may hold values from 0 to 1023, as said below
- ray_slot: int32 [4, 131072], P(None, ('plane', 'ray')), may hold values from 0 to 511, as said below
- fine_cell: int32 [4, 131072], P(None, ('plane', 'ray')), may hold values from 17 to 221, as said below
- coarse_cell: int32 [4, 131072], P(None, ('plane', 'ray')), may hold values from 0 to 262143
- tile_root: int32 [4, 131072], P(None, ('plane', 'ray')), may hold values from 0 to 3
- ray_offset: float32 [2, 131072], P(None, ('plane', 'ray')), may hold values from 0 to 1
Outputs:
- displacement: float32 [2, 131072], P(None, ('plane', 'ray'))
- distortion: float32 [4, 131072], P(None, ('plane', 'ray'))
Inputs may be any that keep to these rules, and one draw needn't show every extreme that they name: `tile_requests`: entries are tile indices within one owner's tiles of the plane. `ray_slot`: A ray's slot r * 16 + s names a tile requested by its own bundle from owner r at that plane. `fine_cell`: both coordinates of a ray's fine cell lie in 1 to 13.
All inputs are finite; a program needn't handle non-finite values.
Results may differ from a plain program's by a relative error of at most 0.0026.
Values may be sent and summed in bfloat16 or wider, within the bound.
No kernel may reach another device: no remote copies, remote signals or barrier semaphores. Data moves between devices by JAX's collectives and lax.ppermute only.
A program may use at most 128 MiB of HBM per device.

v0:
```python
import jax
import jax.numpy as jnp
from jax import lax
from jax.sharding import PartitionSpec as P

TP = 16
RATIO = 32
FIRST = 31


def tile_fields(tiles):
    padded = jnp.pad(tiles, ((0, 0), (1, 1), (1, 1)))
    right_val = padded[:, 1:-1, 2:]
    left_val = padded[:, 1:-1, :-2]
    upper_val = padded[:, 2:, 1:-1]
    lower_val = padded[:, :-2, 1:-1]
    grad_x = (right_val - left_val) * 0.5
    grad_y = (upper_val - lower_val) * 0.5
    hess_xx = right_val - 2.0 * tiles + left_val
    hess_yy = upper_val - 2.0 * tiles + lower_val
    hess_xy = (
        padded[:, 2:, 2:] - padded[:, :-2, 2:] - padded[:, 2:, :-2] + padded[:, :-2, :-2]
    ) * 0.25
    return jnp.stack([grad_x, grad_y, hess_xx, hess_yy, hess_xy], axis=1)


def coarse_terms(plane_rows, coarse_row, fine_row, root_row, position, coarse_side):
    cell_x = coarse_row % coarse_side
    cell_y = coarse_row // coarse_side
    root_x = (root_row % 2 * (RATIO // 2)).astype(jnp.float32)
    root_y = (root_row // 2 * (RATIO // 2)).astype(jnp.float32)
    frac_x = (root_x + (fine_row % TP).astype(jnp.float32) + position[0]) / RATIO
    frac_y = (root_y + (fine_row // TP).astype(jnp.float32) + position[1]) / RATIO
    column_ids = jnp.arange(coarse_side, dtype=jnp.int32)[None, :]
    column_masks = [
        (column_ids == ((cell_x + shift_x) % coarse_side)[:, None]).astype(jnp.float32)
        for shift_x in range(-1, 3)
    ]
    grid_rows = []
    for shift_y in range(-1, 3):
        fetched = jnp.take(plane_rows, (cell_y + shift_y) % coarse_side, axis=0)
        grid_rows.append([jnp.sum(fetched * column_mask, axis=1) for column_mask in column_masks])
    weights = [
        (1.0 - frac_x) * (1.0 - frac_y),
        frac_x * (1.0 - frac_y),
        (1.0 - frac_x) * frac_y,
        frac_x * frac_y,
    ]
    total = jnp.zeros((5, coarse_row.shape[0]), jnp.float32)
    corner_list = ((0, 0), (0, 1), (1, 0), (1, 1))
    for corner_index in range(4):
        step_y = corner_list[corner_index][0] + 1
        step_x = corner_list[corner_index][1] + 1
        middle = grid_rows[step_y][step_x]
        right_val = grid_rows[step_y][step_x + 1]
        left_val = grid_rows[step_y][step_x - 1]
        upper_val = grid_rows[step_y + 1][step_x]
        lower_val = grid_rows[step_y - 1][step_x]
        cross = (
            grid_rows[step_y + 1][step_x + 1]
            - grid_rows[step_y - 1][step_x + 1]
            - grid_rows[step_y + 1][step_x - 1]
            + grid_rows[step_y - 1][step_x - 1]
        ) * 0.25
        stacked = jnp.stack(
            [
                (right_val - left_val) * 0.5,
                (upper_val - lower_val) * 0.5,
                right_val - 2.0 * middle + left_val,
                upper_val - 2.0 * middle + lower_val,
                cross,
            ]
        )
        total = total + weights[corner_index] * stacked
    scales = jnp.array(
        [
            1.0 / RATIO,
            1.0 / RATIO,
            1.0 / (RATIO * RATIO),
            1.0 / (RATIO * RATIO),
            1.0 / (RATIO * RATIO),
        ],
        jnp.float32,
    )
    return total * scales[:, None]


def advance(displacement, previous, distortion, before, deriv, plane_index):
    chi_now = float(FIRST + plane_index)
    ahead = 2.0 * chi_now / (chi_now + 1.0)
    behind = (chi_now - 1.0) / (chi_now + 1.0)
    strength = chi_now / (chi_now + 1.0)
    grad_x, grad_y, hess_xx, hess_yy, hess_xy = (deriv[0], deriv[1], deriv[2], deriv[3], deriv[4])
    new_disp = ahead * displacement - behind * previous - strength * jnp.stack([grad_x, grad_y])
    product = jnp.stack(
        [
            hess_xx * distortion[0] + hess_xy * distortion[2],
            hess_xx * distortion[1] + hess_xy * distortion[3],
            hess_xy * distortion[0] + hess_yy * distortion[2],
            hess_xy * distortion[1] + hess_yy * distortion[3],
        ]
    )
    new_dist = ahead * distortion - behind * before - strength * product
    return (new_disp, displacement, new_dist, distortion)


def fine_block(fields_flat, slot_row, cell_row, position):
    cand_count = fields_flat.shape[0]
    rows_here = slot_row.shape[0]
    tile_cells = TP * TP
    onehot = (slot_row[:, None] == jnp.arange(cand_count, dtype=jnp.int32)[None, :]).astype(
        jnp.bfloat16
    )
    picked = jnp.dot(onehot, fields_flat, preferred_element_type=jnp.float32).reshape(
        rows_here, 5, tile_cells
    )
    cell_ids = jnp.arange(tile_cells, dtype=jnp.int32)[None, :]
    along_x = position[0][:, None]
    along_y = position[1][:, None]
    anchor = cell_row[:, None]
    weights = (
        (1.0 - along_x) * (1.0 - along_y) * (cell_ids == anchor).astype(jnp.float32)
        + along_x * (1.0 - along_y) * (cell_ids == anchor + 1).astype(jnp.float32)
        + (1.0 - along_x) * along_y * (cell_ids == anchor + TP).astype(jnp.float32)
        + along_x * along_y * (cell_ids == anchor + TP + 1).astype(jnp.float32)
    )
    return jnp.einsum("bcn,bn->cb", picked, weights)


def body(
    coarse_potential,
    fine_tiles,
    tile_requests,
    ray_slot,
    fine_cell,
    coarse_cell,
    tile_root,
    ray_offset,
):
    planes = lax.axis_size("plane")
    owners = lax.axis_size("ray")
    slot_count = tile_requests.shape[3]
    coarse_side = coarse_potential.shape[1]
    count_rays = ray_offset.shape[1]
    tile_cells = TP * TP
    requests_local = tile_requests.reshape(planes, owners, slot_count)
    wanted_ids = lax.all_to_all(
        requests_local.reshape(planes * owners, slot_count),
        ("plane", "ray"),
        split_axis=0,
        concat_axis=0,
        tiled=True,
    )
    outgoing = jnp.take(fine_tiles[0], wanted_ids.reshape(-1), axis=0).reshape(
        planes, owners, slot_count, tile_cells
    )
    arrived = lax.all_to_all(
        outgoing.reshape(planes * owners, slot_count, tile_cells),
        ("plane", "ray"),
        split_axis=0,
        concat_axis=0,
        tiled=True,
    )
    arrived = arrived.reshape(planes, owners * slot_count, TP, TP)
    whole_rows = lax.all_gather(coarse_potential, ("plane", "ray"), axis=0, tiled=True)
    displacement = jnp.zeros((2, count_rays), jnp.float32)
    previous = displacement
    ones_row = jnp.ones((count_rays,), jnp.float32)
    zero_row = jnp.zeros((count_rays,), jnp.float32)
    distortion = jnp.stack([ones_row, zero_row, zero_row, ones_row])
    before = distortion
    block_rows = min(512, count_rays)
    block_total = count_rays // block_rows
    for plane_index in range(planes):
        position = ray_offset + displacement
        plane_rows = whole_rows[plane_index * coarse_side : (plane_index + 1) * coarse_side]
        coarse_part = coarse_terms(
            plane_rows,
            coarse_cell[plane_index],
            fine_cell[plane_index],
            tile_root[plane_index],
            position,
            coarse_side,
        )
        fields_flat = (
            tile_fields(arrived[plane_index].astype(jnp.float32))
            .astype(jnp.bfloat16)
            .reshape(-1, 5 * tile_cells)
        )

        def run_block(pieces):
            return fine_block(fields_flat, pieces[0], pieces[1], pieces[2])

        fine_blocks = lax.map(
            run_block,
            (
                ray_slot[plane_index].reshape(block_total, block_rows),
                fine_cell[plane_index].reshape(block_total, block_rows),
                position.reshape(2, block_total, block_rows).transpose(1, 0, 2),
            ),
        )
        fine_part = fine_blocks.transpose(1, 0, 2).reshape(5, count_rays)
        displacement, previous, distortion, before = advance(
            displacement, previous, distortion, before, fine_part + coarse_part, plane_index
        )
    return (displacement, distortion)


def solution(mesh):
    in_specs = (
        P(("plane", "ray"), None),
        P("plane", "ray", None),
        P(("plane", "ray"), None, None, None),
        P(None, ("plane", "ray")),
        P(None, ("plane", "ray")),
        P(None, ("plane", "ray")),
        P(None, ("plane", "ray")),
        P(None, ("plane", "ray")),
    )
    out_specs = (P(None, ("plane", "ray")), P(None, ("plane", "ray")))
    return jax.shard_map(body, mesh=mesh, in_specs=in_specs, out_specs=out_specs, check_vma=False)
```

profile of v0, /device:TPU:1, one launch (start us, length us, event | category | flops | bytes accessed | tf_op | source)
XLA Modules:
  0.0 516.5 jit_solution(14348921904441071178)
XLA Ops:
  8.7 11.5 %all-to-all-start = ((s32[128,1,16]{2,1,0:T(1,128)}), s32[128,1,16]{2,1,0:T(1,128)S(1)}, u32[]{:S(2)}, u32[]{:S(2)}) async-start(s32[128,1,16]{2,1,0:T(1,128)} %bitcast.38), calls=%async_computation | async-start | bytes 131072 | tf_op jit(solution)/shard_map/all_to_all | solution.py:147
  31.3 7.5 %gather_fusion = bf16[2048,256]{1,0:T(8,128)(2,1)S(1)} fusion(bf16[1024,256]{1,0:T(8,128)(2,1)S(1)} %bitcast.261, s32[2048]{0:T(1024)S(1)} %broadcast_clamp_fusion), kind=kCustom, calls=%fused_computation.16 | custom fusion | bytes 2105344 | tf_op jit(solution)/shard_map/jit(_take)/gather | solution.py:154
  40.1 9.5 %all-to-all-start.1 = ((bf16[128,16,256]{2,1,0:T(8,128)(2,1)}), bf16[128,16,256]{2,1,0:T(8,128)(2,1)S(1)}, u32[]{:S(2)}, u32[]{:S(2)}) async-start(bf16[128,16,256]{2,1,0:T(8,128)(2,1)} %broadcast_select_fusion), calls=%async_computation.1 | async-start | bytes 2097152 | tf_op jit(solution)/shard_map/all_to_all | solution.py:157
  52.3 17.2 %all-to-all-done.1 = bf16[128,16,256]{2,1,0:T(8,128)(2,1)S(1)} async-done(((bf16[128,16,256]{2,1,0:T(8,128)(2,1)}), bf16[128,16,256]{2,1,0:T(8,128)(2,1)S(1)}, u32[]{:S(2)}, u32[]{:S(2)}) %all-to-all-start.1) | async-done | bytes 1048608 | tf_op jit(solution)/shard_map/all_to_all | solution.py:157
  73.2 31.9 %fusion.47 = (bf16[512,1,16,16]{3,2,0,1:T(8,128)(2,1)S(1)}, bf16[512,1,16,16]{3,2,0,1:T(8,128)(2,1)}, bf16[512,1,16,16]{3,2,0,1:T(8,128)(2,1)}, bf16[512,1,16,16]{3,2,0,1:T(8,128)(2,1)}, bf16[512,1,16,16]{3,2,0,1:T(8,128)(2,1)}) fusion(f32[512,16,16]{2,1,0:T(8,128)} %reshape.2442), kind=kLoop, calls=%fused_computation.264 | loop fusion | flops 2359296 | bytes 1835008 | tf_op jit(solution)/shard_map/stack | solution.py:24
  130.2 32.1 %fusion.46 = (bf16[512,1,16,16]{3,2,0,1:T(8,128)(2,1)S(1)}, bf16[512,1,16,16]{3,2,0,1:T(8,128)(2,1)}, bf16[512,1,16,16]{3,2,0,1:T(8,128)(2,1)}, bf16[512,1,16,16]{3,2,0,1:T(8,128)(2,1)}, bf16[512,1,16,16]{3,2,0,1:T(8,128)(2,1)}) fusion(f32[512,16,16]{2,1,0:T(8,128)} %reshape.2443), kind=kLoop, calls=%fused_computation.263 | loop fusion | flops 2359296 | bytes 1835008 | tf_op jit(solution)/shard_map/stack | solution.py:24
  183.5 31.9 %fusion.45 = (bf16[512,1,16,16]{3,2,0,1:T(8,128)(2,1)S(1)}, bf16[512,1,16,16]{3,2,0,1:T(8,128)(2,1)}, bf16[512,1,16,16]{3,2,0,1:T(8,128)(2,1)}, bf16[512,1,16,16]{3,2,0,1:T(8,128)(2,1)}, bf16[512,1,16,16]{3,2,0,1:T(8,128)(2,1)}) fusion(f32[512,16,16]{2,1,0:T(8,128)} %reshape.2444), kind=kLoop, calls=%fused_computation.262 | loop fusion | flops 2359296 | bytes 1835008 | tf_op jit(solution)/shard_map/stack | solution.py:24
  234.6 31.9 %fusion.44 = (bf16[512,1,16,16]{3,2,0,1:T(8,128)(2,1)S(1)}, bf16[512,1,16,16]{3,2,0,1:T(8,128)(2,1)}, bf16[512,1,16,16]{3,2,0,1:T(8,128)(2,1)}, bf16[512,1,16,16]{3,2,0,1:T(8,128)(2,1)}, bf16[512,1,16,16]{3,2,0,1:T(8,128)(2,1)}) fusion(f32[512,16,16]{2,1,0:T(8,128)} %reshape.2445), kind=kLoop, calls=%fused_computation.261 | loop fusion | flops 2359296 | bytes 1835008 | tf_op jit(solution)/shard_map/stack | solution.py:24
  279.7 11.4 %while.48 = (s32[]{:T(128)}, f32[2,5,512]{2,1,0:T(8,128)S(1)}, s32[2,512]{1,0:T(2,128)S(1)}, f32[2,2,512]{2,1,0:T(2,128)S(1)}, s32[2,512]{1,0:T(2,128)S(1)}, /*i...) while((s32[]{:T(128)}, f32[2,5,512]{2,1,0:T(8,128)S(1)}, s32[2,512]{1,0:T(2,128)S(1)}, ...), condition=%wide.region_1.2_spmd, body=%wide.region_0.1_spmd.sunk | while | flops 674105344 | bytes 8749185 | solution.py:194
  291.1 39.7 %all-gather.2.cloned.1.call-done = f32[2048,512]{1,0:T(8,128)} async-done(((f32[16,512]{1,0:T(8,128)}), f32[2048,512]{1,0:T(8,128)}) %all-gather.2.cloned.1.call-update) | async-done | bytes 4194320 | tf_op jit(solution)/shard_map/all_gather | solution.py:165
  334.4 6.5 %gather_fusion.2 = f32[1024,512]{1,0:T(8,128)} fusion(f32[512,512]{1,0:T(8,128)} %get-tuple-element.600, s32[1024]{0:T(1024)S(1)} %get-tuple-element.791), kind=kCustom, calls=%fused_computation.1.clone | custom fusion | bytes 4198400 | tf_op jit(solution)/shard_map/jit(_take)/gather | solution.py:41
  340.9 6.5 %gather_fusion.3 = f32[1024,512]{1,0:T(8,128)} fusion(f32[512,512]{1,0:T(8,128)} %get-tuple-element.600, s32[1024]{0:T(1024)S(1)} %get-tuple-element.790), kind=kCustom, calls=%fused_computation.2.clone | custom fusion | bytes 4198400 | tf_op jit(solution)/shard_map/jit(_take)/gather | solution.py:41
  347.5 6.5 %gather_fusion.4 = f32[1024,512]{1,0:T(8,128)} fusion(f32[512,512]{1,0:T(8,128)} %get-tuple-element.600, s32[1024]{0:T(1024)S(1)} %get-tuple-element.789), kind=kCustom, calls=%fused_computation.3.clone | custom fusion | bytes 4198400 | tf_op jit(solution)/shard_map/jit(_take)/gather | solution.py:41
  354.0 6.5 %gather_fusion.1 = f32[1024,512]{1,0:T(8,128)} fusion(f32[512,512]{1,0:T(8,128)} %get-tuple-element.600, s32[1024]{0:T(1024)S(1)} %get-tuple-element.792), kind=kCustom, calls=%fused_computation.clone | custom fusion | bytes 4198400 | tf_op jit(solution)/shard_map/jit(_take)/gather | solution.py:41
  360.6 9.5 %select_reduce_fusion.56 = (f32[1024]{0:T(1024)S(1)}, f32[1024]{0:T(1024)S(1)}, f32[1024]{0:T(1024)S(1)}, f32[1024]{0:T(1024)S(1)}, f32[1024]{0:T(1024)S(1)}, /*...) fusion(f32[1024,512]{1,0:T(8,128)} %gather_fusion.2, ...), kind=kLoop, calls=%fused_computation.250 | loop fusion | flops 20955136 | bytes 8474624 | tf_op jit(solution)/shard_map/reduce_sum | solution.py:42
  371.9 19.3 %while.49 = (s32[]{:T(128)}, f32[2,5,512]{2,1,0:T(8,128)S(1)}, s32[2,512]{1,0:T(2,128)S(1)}, f32[2,2,512]{2,1,0:T(2,128)S(1)}, s32[2,512]{1,0:T(2,128)S(1)}, /*i...) while((s32[]{:T(128)}, f32[2,5,512]{2,1,0:T(8,128)S(1)}, s32[2,512]{1,0:T(2,128)S(1)}, ...), condition=%wide.region_19.21_spmd, body=%wide.region_18.20_spmd.sunk | while | flops 674105344 | bytes 8749185 | solution.py:194
  391.2 4.9 gather_fusion.6
  396.1 4.9 gather_fusion.7
  401.0 4.9 gather_fusion.8
  405.9 4.9 gather_fusion.5
  410.9 9.5 %select_reduce_fusion.40 = (f32[1024]{0:T(1024)S(1)}, f32[1024]{0:T(1024)S(1)}, f32[1024]{0:T(1024)S(1)}, f32[1024]{0:T(1024)S(1)}, f32[1024]{0:T(1024)S(1)}, /*...) fusion(f32[1024,512]{1,0:T(8,128)} %gather_fusion.6, ...), kind=kLoop, calls=%fused_computation.230 | loop fusion | flops 20955136 | bytes 8474624 | tf_op jit(solution)/shard_map/reduce_sum | solution.py:42
  421.5 14.0 %while.50 = (s32[]{:T(128)}, f32[2,5,512]{2,1,0:T(8,128)S(1)}, s32[2,512]{1,0:T(2,128)S(1)}, f32[2,2,512]{2,1,0:T(2,128)S(1)}, s32[2,512]{1,0:T(2,128)S(1)}, /*i...) while((s32[]{:T(128)}, f32[2,5,512]{2,1,0:T(8,128)S(1)}, s32[2,512]{1,0:T(2,128)S(1)}, ...), condition=%wide.region_37.39_spmd, body=%wide.region_36.38_spmd.sunk | while | flops 674105344 | bytes 8749185 | solution.py:194
  435.4 4.9 gather_fusion.10
  440.3 4.9 gather_fusion.11
  445.2 4.9 gather_fusion.12
  450.2 4.9 gather_fusion.9
  455.2 9.6 %select_reduce_fusion.24 = (f32[1024]{0:T(1024)S(1)}, f32[1024]{0:T(1024)S(1)}, f32[1024]{0:T(1024)S(1)}, f32[1024]{0:T(1024)S(1)}, f32[1024]{0:T(1024)S(1)}, /*...) fusion(f32[1024,512]{1,0:T(8,128)} %gather_fusion.10, ...), kind=kLoop, calls=%fused_computation.210 | loop fusion | flops 20955136 | bytes 8474624 | tf_op jit(solution)/shard_map/reduce_sum | solution.py:42
  467.3 12.5 %while.51 = (s32[]{:T(128)}, f32[2,5,512]{2,1,0:T(8,128)S(1)}, s32[2,512]{1,0:T(2,128)}, f32[2,2,512]{2,1,0:T(2,128)S(1)}, s32[2,512]{1,0:T(2,128)}, /*index=5*/...) while((s32[]{:T(128)}, f32[2,5,512]{2,1,0:T(8,128)S(1)}, s32[2,512]{1,0:T(2,128)}, ...), condition=%wide.region_55.57_spmd, body=%wide.region_54.56_spmd.sunk | while | flops 674105344 | bytes 8749185 | solution.py:194
  483.3 4.9 gather_fusion.15
  488.2 4.9 gather_fusion.16
  493.3 4.9 gather_fusion.13
  498.6 9.2 %select_reduce_fusion.8 = (f32[1024]{0:T(1024)S(1)}, f32[1024]{0:T(1024)S(1)}, f32[1024]{0:T(1024)S(1)}, f32[1024]{0:T(1024)S(1)}, f32[1024]{0:T(1024)S(1)}, /*i...) fusion(f32[1024,512]{1,0:T(8,128)S(1)} %gather_fusion.14, ...), kind=kLoop, calls=%fused_computation.190 | loop fusion | flops 20955136 | bytes 8474624 | tf_op jit(solution)/shard_map/reduce_sum | solution.py:42
  (310 shorter events, 169.3 us)
Async XLA Ops:
  7.2 24.1 %copy-start = (bf16[1,1024,256]{2,1,0:T(8,128)(2,1)S(1)}, bf16[1,1024,256]{2,1,0:T(8,128)(2,1)}, u32[]{:S(2)}) copy-start(bf16[1,1024,256]{2,1,0:T(8,128)(2,1)} %param.23) | copy-start | bytes 1572868
  8.7 21.1 %all-to-all-start = ((s32[128,1,16]{2,1,0:T(1,128)}), s32[128,1,16]{2,1,0:T(1,128)S(1)}, u32[]{:S(2)}, u32[]{:S(2)}) async-start(s32[128,1,16]{2,1,0:T(1,128)} %bitcast.38), calls=%async_computation | async-start | bytes 131072 | tf_op jit(solution)/shard_map/all_to_all | solution.py:147
  20.2 310.6 %all-gather.2.cloned.1.call-start = ((), (), s32[]{:S(2)}) async-start(), calls=%async_computation.2 | async-start | bytes 4227072 | tf_op jit(solution)/shard_map/all_gather | solution.py:165
  38.8 11.4 %copy-start.5 = (f32[2,1024]{1,0:T(2,128)S(1)}, f32[2,1024]{1,0:T(2,128)}, u32[]{:S(2)}) copy-start(f32[2,1024]{1,0:T(2,128)} %param.29) | copy-start | bytes 24580
  38.8 11.4 %copy-start.11 = (s32[4,1024]{1,0:T(4,128)S(1)}, s32[4,1024]{1,0:T(4,128)}, u32[]{:S(2)}) copy-start(s32[4,1024]{1,0:T(4,128)} %param.26) | copy-start | bytes 49156
  40.1 29.4 %all-to-all-start.1 = ((bf16[128,16,256]{2,1,0:T(8,128)(2,1)}), bf16[128,16,256]{2,1,0:T(8,128)(2,1)S(1)}, u32[]{:S(2)}, u32[]{:S(2)}) async-start(bf16[128,16,256]{2,1,0:T(8,128)(2,1)} %broadcast_select_fusion), calls=%async_computation.1 | async-start | bytes 2097152 | tf_op jit(solution)/shard_map/all_to_all | solution.py:157
  121.0 6.6 %copy-start.2 = (f32[32,16,256]{2,1,0:T(8,128)S(1)}, f32[32,16,256]{2,1,0:T(8,128)}, u32[]{:S(2)}) copy-start(f32[32,16,256]{2,1,0:T(8,128)} %get-tuple-element.623) | copy-start | bytes 1572868
  354.0 6.5 %copy-start.48 = (pred[1024]{0:T(1024)(128)(4,1)S(1)}, pred[1024]{0:T(1024)(128)(4,1)}, u32[]{:S(2)}) copy-start(pred[1024]{0:T(1024)(128)(4,1)} %get-tuple-element.551) | copy-start | bytes 3076
  354.0 6.5 %copy-start.49 = (pred[1024]{0:T(1024)(128)(4,1)S(1)}, pred[1024]{0:T(1024)(128)(4,1)}, u32[]{:S(2)}) copy-start(pred[1024]{0:T(1024)(128)(4,1)} %get-tuple-element.774) | copy-start | bytes 3076
  354.0 6.5 %copy-start.50 = (pred[1024]{0:T(1024)(128)(4,1)S(1)}, pred[1024]{0:T(1024)(128)(4,1)}, u32[]{:S(2)}) copy-start(pred[1024]{0:T(1024)(128)(4,1)} %get-tuple-element.775) | copy-start | bytes 3076
  354.0 6.5 %copy-start.51 = (pred[1024]{0:T(1024)(128)(4,1)S(1)}, pred[1024]{0:T(1024)(128)(4,1)}, u32[]{:S(2)}) copy-start(pred[1024]{0:T(1024)(128)(4,1)} %get-tuple-element.776) | copy-start | bytes 3076
  360.6 9.8 %copy-start.30 = (f32[1,1024]{1,0:T(1,128)S(1)}, f32[1,1024]{1,0:T(1,128)}, u32[]{:S(2)}) copy-start(f32[1,1024]{1,0:T(1,128)} %get-tuple-element.714) | copy-start | bytes 12292
  360.6 11.2 %copy-start.26 = (s32[4,1024]{1,0:T(4,128)S(1)}, s32[4,1024]{1,0:T(4,128)}, u32[]{:S(2)}) copy-start(s32[4,1024]{1,0:T(4,128)} %param.28) | copy-start | bytes 49156
  410.9 9.8 %copy-start.33 = (f32[5]{0:T(128)S(1)}, f32[5]{0:T(128)}, u32[]{:S(2)}) copy-start(f32[5]{0:T(128)} %constant.668.clone) | copy-start | bytes 64
  455.2 9.9 %copy-start.32 = (f32[1,1024]{1,0:T(1,128)S(1)}, f32[1,1024]{1,0:T(1,128)}, u32[]{:S(2)}) copy-start(f32[1,1024]{1,0:T(1,128)} %get-tuple-element.538) | copy-start | bytes 12292
  455.2 9.9 %copy-start.34 = (f32[5]{0:T(128)S(1)}, f32[5]{0:T(128)}, u32[]{:S(2)}) copy-start(f32[5]{0:T(128)} %constant.668.clone) | copy-start | bytes 64
  455.2 12.0 %copy-start.3 = (bf16[512,1280]{1,0:T(8,128)(2,1)S(1)}, bf16[512,1280]{1,0:T(8,128)(2,1)}, u32[]{:S(2)}) copy-start(bf16[512,1280]{1,0:T(8,128)(2,1)} %copy.85) | copy-start | bytes 3932164
  467.2 12.6 %copy-start.20 = (s32[1024]{0:T(1024)S(1)}, s32[1024]{0:T(1024)}, u32[]{:S(2)}) copy-start(s32[1024]{0:T(1024)} %get-tuple-element.738) | copy-start | bytes 12292
  493.2 5.2 %copy-start.28 = (f32[1,1024]{1,0:T(1,128)S(1)}, f32[1,1024]{1,0:T(1,128)}, u32[]{:S(2)}) copy-start(f32[1,1024]{1,0:T(1,128)} %get-tuple-element.532) | copy-start | bytes 12292
  493.2 5.2 %copy-start.29 = (f32[1,1024]{1,0:T(1,128)S(1)}, f32[1,1024]{1,0:T(1,128)}, u32[]{:S(2)}) copy-start(f32[1,1024]{1,0:T(1,128)} %get-tuple-element.533) | copy-start | bytes 12292
  493.2 5.2 %copy-start.13 = (s32[1024]{0:T(1024)S(1)}, s32[1024]{0:T(1024)}, u32[]{:S(2)}) copy-start(s32[1024]{0:T(1024)} %get-tuple-element.744) | copy-start | bytes 12292
  493.2 5.2 %copy-start.14 = (s32[1024]{0:T(1024)S(1)}, s32[1024]{0:T(1024)}, u32[]{:S(2)}) copy-start(s32[1024]{0:T(1024)} %get-tuple-element.745) | copy-start | bytes 12292
  493.3 5.2 %copy-start.15 = (s32[1024]{0:T(1024)S(1)}, s32[1024]{0:T(1024)}, u32[]{:S(2)}) copy-start(s32[1024]{0:T(1024)} %get-tuple-element.746) | copy-start | bytes 12292
  493.3 5.2 %copy-start.16 = (s32[1024]{0:T(1024)S(1)}, s32[1024]{0:T(1024)}, u32[]{:S(2)}) copy-start(s32[1024]{0:T(1024)} %get-tuple-element.747) | copy-start | bytes 12292
  493.3 5.2 %copy-start.36 = (pred[1024]{0:T(1024)(128)(4,1)S(1)}, pred[1024]{0:T(1024)(128)(4,1)}, u32[]{:S(2)}) copy-start(pred[1024]{0:T(1024)(128)(4,1)} %get-tuple-element.534) | copy-start | bytes 3076
  493.3 5.2 %copy-start.37 = (pred[1024]{0:T(1024)(128)(4,1)S(1)}, pred[1024]{0:T(1024)(128)(4,1)}, u32[]{:S(2)}) copy-start(pred[1024]{0:T(1024)(128)(4,1)} %get-tuple-element.741) | copy-start | bytes 3076
  493.3 5.2 %copy-start.38 = (pred[1024]{0:T(1024)(128)(4,1)S(1)}, pred[1024]{0:T(1024)(128)(4,1)}, u32[]{:S(2)}) copy-start(pred[1024]{0:T(1024)(128)(4,1)} %get-tuple-element.742) | copy-start | bytes 3076
  493.3 5.2 %copy-start.39 = (pred[1024]{0:T(1024)(128)(4,1)S(1)}, pred[1024]{0:T(1024)(128)(4,1)}, u32[]{:S(2)}) copy-start(pred[1024]{0:T(1024)(128)(4,1)} %get-tuple-element.743) | copy-start | bytes 3076
  498.5 9.5 %copy-start.31 = (f32[1,1024]{1,0:T(1,128)S(1)}, f32[1,1024]{1,0:T(1,128)}, u32[]{:S(2)}) copy-start(f32[1,1024]{1,0:T(1,128)} %get-tuple-element.531) | copy-start | bytes 12292
  498.5 9.5 %copy-start.35 = (f32[5]{0:T(128)S(1)}, f32[5]{0:T(128)}, u32[]{:S(2)}) copy-start(f32[5]{0:T(128)} %constant.668.clone) | copy-start | bytes 64
  498.6 9.6 %copy-start.12 = (f32[2,1024]{1,0:T(2,128)S(1)}, f32[2,1024]{1,0:T(2,128)}, u32[]{:S(2)}) copy-start(f32[2,1024]{1,0:T(2,128)} %get-tuple-element.537) | copy-start | bytes 24580
  498.6 10.9 %copy-start.1 = (bf16[1,1024,256]{2,1,0:T(8,128)(2,1)S(1)}, bf16[1,1024,256]{2,1,0:T(8,128)(2,1)}, u32[]{:S(2)}) copy-start(bf16[1,1024,256]{2,1,0:T(8,128)(2,1)} %param.23) | copy-start | bytes 1572868
  (23 other events, 111.4 us)
Sparse Core Ops, SparseCore 0:
  22.7 308.0 all-gather.1
where the time goes:
time: 527 us; the launch traced here: 517 us
  other arithmetic  206 us (39%)
  local copies, waits for them, and re-layouts  190 us (36%)
  waiting for transfers between devices  57.8 us (11%)
  matrix products  25.3 us (5%)
  starting transfers between devices  21.1 us (4%)
  between operations  15.2 us (3%)
    another operation x4, other arithmetic, tile_fields(): return jnp.stack([grad_x, grad_y, hess_xx, hess_yy, hess_xy], axis=1)  128 us
    gather x16, local copies, waits for them, and re-layouts, coarse_terms(): fetched = jnp.take(plane_rows, (cell_y + shift_y) % coarse_side, axis=0)  83.5 us
    another operation x24, local copies, waits for them, and re-layouts, tile_fields(): return jnp.stack([grad_x, grad_y, hess_xx, hess_yy, hess_xy], axis=1)  53.9 us
    all_gather x1, waiting for transfers between devices, body(): lax.all_gather(coarse_potential, ('plane', 'ray'), axis=0, tiled=True)  39.7 us
    reduce_sum x4, other arithmetic, coarse_terms(): jnp.sum(fetched * column_mask, axis=1)  37.7 us
    dot_general x8, matrix products, fine_block(): jnp.dot(onehot, fields_flat, preferred_element_type=jnp.float32)  25.3 us
    all_to_all x1, waiting for transfers between devices, body(): lax.all_to_all(outgoing.reshape(planes * owners, slot_count, tile_cells),...  17.2 us
    dot_general x8, other arithmetic, fine_block(): return jnp.einsum('bcn,bn->cb', picked, weights)  15.8 us
  transfers between devices with their start and end apart: 3, of which 3 were waited for; matrix products, arithmetic and copies ran while one was open for 47% of the time, Pallas kernels for 0%

commit v1 on v0

--- a/solution.py
+++ b/solution.py
@@ -162,7 +162,12 @@
         tiled=True,
     )
     arrived = arrived.reshape(planes, owners * slot_count, TP, TP)
-    whole_rows = lax.all_gather(coarse_potential, ("plane", "ray"), axis=0, tiled=True)
+    whole_rows = jnp.concatenate(
+        lax.all_to_all(
+            jnp.stack([coarse_potential] * lax.axis_size(("plane", "ray"))), ("plane", "ray"), 0, 0
+        ),
+        axis=0,
+    )
     displacement = jnp.zeros((2, count_rays), jnp.float32)
     previous = displacement
     ones_row = jnp.ones((count_rays,), jnp.float32)

time: 527 us -> 493 us (0.935)
  waiting for transfers between devices: 57.8 us -> 15.8 us
  between operations: 15.2 us -> 2.01 us
  local copies, waits for them, and re-layouts: 190 us -> 201 us
  other arithmetic: 206 us -> 216 us
  starting transfers between devices: 21.1 us -> 26.8 us
    all_gather x1 -> x0, waiting for transfers between devices: 39.7 us -> none  [body(): lax.all_gather(coarse_potential, ('plane', 'ray'), axis=0, tiled=True)]
    another operation x4, other arithmetic: 128 us -> 136 us  [tile_fields(): return jnp.stack([grad_x, grad_y, hess_xx, hess_yy, hess_xy], axis=1)]
    all_to_all x0 -> x1, starting transfers between devices: none -> 5.93 us  [body(): lax.all_to_all(jnp.stack([coarse_potential] * lax.axis_size(('plane', 'ra...]
    unnamed x120 -> x146, local copies, waits for them, and re-layouts: 10.1 us -> 13.7 us
  transfers between devices with their start and end apart: 3 -> 3, of which waited for: 3 -> 2; matrix products, arithmetic and copies ran while one was open for 47% -> 51% of each run, Pallas kernels for 0% -> 0%
where the time goes in v1:
time: 493 us; the launch traced here: 487 us
  other arithmetic  216 us (44%)
  local copies, waits for them, and re-layouts  201 us (41%)
  starting transfers between devices  26.8 us (5%)
  matrix products  25.3 us (5%)
  waiting for transfers between devices  15.8 us (3%)
    another operation x4, other arithmetic, tile_fields(): return jnp.stack([grad_x, grad_y, hess_xx, hess_yy, hess_xy], axis=1)  136 us
    gather x16, local copies, waits for them, and re-layouts, coarse_terms(): fetched = jnp.take(plane_rows, (cell_y + shift_y) % coarse_side, axis=0)  83.5 us
    another operation x24, local copies, waits for them, and re-layouts, tile_fields(): return jnp.stack([grad_x, grad_y, hess_xx, hess_yy, hess_xy], axis=1)  57.1 us
    reduce_sum x4, other arithmetic, coarse_terms(): jnp.sum(fetched * column_mask, axis=1)  37.8 us
    dot_general x8, matrix products, fine_block(): jnp.dot(onehot, fields_flat, preferred_element_type=jnp.float32)  25.3 us
    dot_general x8, other arithmetic, fine_block(): return jnp.einsum('bcn,bn->cb', picked, weights)  15.8 us
    all_to_all x1, waiting for transfers between devices, body(): lax.all_to_all(outgoing.reshape(planes * owners, slot_count, tile_cells),...  15.4 us
    unnamed x146, local copies, waits for them, and re-layouts  13.7 us
  transfers between devices with their start and end apart: 3, of which 2 were waited for; matrix products, arithmetic and copies ran while one was open for 51% of the time, Pallas kernels for 0%

profile of v1, /device:TPU:1, one launch (start us, length us, event | category | flops | bytes accessed | tf_op | source)
XLA Modules:
  0.0 487.1 jit_solution(8249550944642795958)
XLA Ops:
  2.2 11.5 %all-to-all-start = ((s32[128,1,16]{2,1,0:T(1,128)}), s32[128,1,16]{2,1,0:T(1,128)S(1)}, u32[]{:S(2)}, u32[]{:S(2)}) async-start(s32[128,1,16]{2,1,0:T(1,128)} %bitcast.38), calls=%async_computation | async-start | bytes 131072 | tf_op jit(solution)/shard_map/all_to_all | solution.py:147
  24.8 7.5 %gather_fusion = bf16[2048,256]{1,0:T(8,128)(2,1)S(1)} fusion(bf16[1024,256]{1,0:T(8,128)(2,1)S(1)} %bitcast.265, s32[2048]{0:T(1024)S(1)} %broadcast_clamp_fusion), kind=kCustom, calls=%fused_computation.16 | custom fusion | bytes 2105344 | tf_op jit(solution)/shard_map/jit(_take)/gather | solution.py:154
  33.5 9.4 %all-to-all-start.1 = ((bf16[128,16,256]{2,1,0:T(8,128)(2,1)}), bf16[128,16,256]{2,1,0:T(8,128)(2,1)S(1)}, u32[]{:S(2)}, u32[]{:S(2)}) async-start(bf16[128,16,256]{2,1,0:T(8,128)(2,1)} %broadcast_select_fusion), calls=%async_computation.1 | async-start | bytes 2097152 | tf_op jit(solution)/shard_map/all_to_all | solution.py:157
  46.8 15.4 %all-to-all-done.1 = bf16[128,16,256]{2,1,0:T(8,128)(2,1)S(1)} async-done(((bf16[128,16,256]{2,1,0:T(8,128)(2,1)}), bf16[128,16,256]{2,1,0:T(8,128)(2,1)S(1)}, u32[]{:S(2)}, u32[]{:S(2)}) %all-to-all-start.1) | async-done | bytes 1048608 | tf_op jit(solution)/shard_map/all_to_all | solution.py:157
  64.7 5.9 %all-to-all-start.2 = ((f32[128,16,512]{2,1,0:T(8,128)}), f32[128,16,512]{2,1,0:T(8,128)}, u32[]{:S(2)}, u32[]{:S(2)}) async-start(f32[128,16,512]{2,1,0:T(8,128)} %stack.128), calls=%async_computation.2 | async-start | bytes 8388608 | tf_op jit(solution)/shard_map/all_to_all | solution.py:166
  74.3 33.9 %fusion.47 = (bf16[512,1,16,16]{3,2,0,1:T(8,128)(2,1)S(1)}, bf16[512,1,16,16]{3,2,0,1:T(8,128)(2,1)}, bf16[512,1,16,16]{3,2,0,1:T(8,128)(2,1)}, bf16[512,1,16,16]{3,2,0,1:T(8,128)(2,1)}, bf16[512,1,16,16]{3,2,0,1:T(8,128)(2,1)}) fusion(f32[512,16,16]{2,1,0:T(8,128)} %reshape.2449), kind=kLoop, calls=%fused_computation.264 | loop fusion | flops 2359296 | bytes 1835008 | tf_op jit(solution)/shard_map/stack | solution.py:24
  133.3 33.9 %fusion.46 = (bf16[512,1,16,16]{3,2,0,1:T(8,128)(2,1)S(1)}, bf16[512,1,16,16]{3,2,0,1:T(8,128)(2,1)}, bf16[512,1,16,16]{3,2,0,1:T(8,128)(2,1)}, bf16[512,1,16,16]{3,2,0,1:T(8,128)(2,1)}, bf16[512,1,16,16]{3,2,0,1:T(8,128)(2,1)}) fusion(f32[512,16,16]{2,1,0:T(8,128)} %reshape.2450), kind=kLoop, calls=%fused_computation.263 | loop fusion | flops 2359296 | bytes 1835008 | tf_op jit(solution)/shard_map/stack | solution.py:24
  192.5 33.9 %fusion.45 = (bf16[512,1,16,16]{3,2,0,1:T(8,128)(2,1)S(1)}, bf16[512,1,16,16]{3,2,0,1:T(8,128)(2,1)}, bf16[512,1,16,16]{3,2,0,1:T(8,128)(2,1)}, bf16[512,1,16,16]{3,2,0,1:T(8,128)(2,1)}, bf16[512,1,16,16]{3,2,0,1:T(8,128)(2,1)}) fusion(f32[512,16,16]{2,1,0:T(8,128)} %reshape.2451), kind=kLoop, calls=%fused_computation.262 | loop fusion | flops 2359296 | bytes 1835008 | tf_op jit(solution)/shard_map/stack | solution.py:24
  243.9 34.3 %fusion.44 = (bf16[512,1,16,16]{3,2,0,1:T(8,128)(2,1)S(1)}, bf16[512,1,16,16]{3,2,0,1:T(8,128)(2,1)}, bf16[512,1,16,16]{3,2,0,1:T(8,128)(2,1)}, bf16[512,1,16,16]{3,2,0,1:T(8,128)(2,1)}, bf16[512,1,16,16]{3,2,0,1:T(8,128)(2,1)}) fusion(f32[512,16,16]{2,1,0:T(8,128)} %reshape.2452), kind=kLoop, calls=%fused_computation.261 | loop fusion | flops 2359296 | bytes 1835008 | tf_op jit(solution)/shard_map/stack | solution.py:24
  296.7 11.0 %while.48 = (s32[]{:T(128)}, f32[2,5,512]{2,1,0:T(8,128)S(1)}, s32[2,512]{1,0:T(2,128)S(1)}, f32[2,2,512]{2,1,0:T(2,128)S(1)}, s32[2,512]{1,0:T(2,128)S(1)}, /*i...) while((s32[]{:T(128)}, f32[2,5,512]{2,1,0:T(8,128)S(1)}, s32[2,512]{1,0:T(2,128)S(1)}, ...), condition=%wide.region_1.2_spmd, body=%wide.region_0.1_spmd.sunk | while | flops 674105344 | bytes 8749185 | solution.py:199
  311.5 6.5 %gather_fusion.2 = f32[1024,512]{1,0:T(8,128)} fusion(f32[512,512]{1,0:T(8,128)} %bitcast.278, s32[1024]{0:T(1024)S(1)} %get-tuple-element.791), kind=kCustom, calls=%fused_computation.1.clone | custom fusion | bytes 4198400 | tf_op jit(solution)/shard_map/jit(_take)/gather | solution.py:41
  318.0 6.5 %gather_fusion.3 = f32[1024,512]{1,0:T(8,128)} fusion(f32[512,512]{1,0:T(8,128)} %bitcast.279, s32[1024]{0:T(1024)S(1)} %get-tuple-element.790), kind=kCustom, calls=%fused_computation.2.clone | custom fusion | bytes 4198400 | tf_op jit(solution)/shard_map/jit(_take)/gather | solution.py:41
  324.6 6.5 %gather_fusion.4 = f32[1024,512]{1,0:T(8,128)} fusion(f32[512,512]{1,0:T(8,128)} %bitcast.280, s32[1024]{0:T(1024)S(1)} %get-tuple-element.789), kind=kCustom, calls=%fused_computation.3.clone | custom fusion | bytes 4198400 | tf_op jit(solution)/shard_map/jit(_take)/gather | solution.py:41
  331.1 6.5 %gather_fusion.1 = f32[1024,512]{1,0:T(8,128)} fusion(f32[512,512]{1,0:T(8,128)} %bitcast.281, s32[1024]{0:T(1024)S(1)} %get-tuple-element.792), kind=kCustom, calls=%fused_computation.clone | custom fusion | bytes 4198400 | tf_op jit(solution)/shard_map/jit(_take)/gather | solution.py:41
  337.8 9.6 %select_reduce_fusion.56 = (f32[1024]{0:T(1024)S(1)}, f32[1024]{0:T(1024)S(1)}, f32[1024]{0:T(1024)S(1)}, f32[1024]{0:T(1024)S(1)}, f32[1024]{0:T(1024)S(1)}, /*...) fusion(f32[1024,512]{1,0:T(8,128)} %gather_fusion.2, ...), kind=kLoop, calls=%fused_computation.250 | loop fusion | flops 20955136 | bytes 8474624 | tf_op jit(solution)/shard_map/reduce_sum | solution.py:42
  349.2 19.3 %while.49 = (s32[]{:T(128)}, f32[2,5,512]{2,1,0:T(8,128)S(1)}, s32[2,512]{1,0:T(2,128)S(1)}, f32[2,2,512]{2,1,0:T(2,128)S(1)}, s32[2,512]{1,0:T(2,128)S(1)}, /*i...) while((s32[]{:T(128)}, f32[2,5,512]{2,1,0:T(8,128)S(1)}, s32[2,512]{1,0:T(2,128)S(1)}, ...), condition=%wide.region_19.21_spmd, body=%wide.region_18.20_spmd.sunk | while | flops 674105344 | bytes 8749185 | solution.py:199
  368.5 4.9 %gather_fusion.6 = f32[1024,512]{1,0:T(8,128)} fusion(f32[512,512]{1,0:T(8,128)S(1)} %bitcast.274, s32[1024]{0:T(1024)S(1)} %copy-done.30), kind=kCustom, calls=%fused_computation.5.clone | custom fusion | bytes 4198400 | tf_op jit(solution)/shard_map/jit(_take)/gather | solution.py:41
  373.4 4.9 %gather_fusion.7 = f32[1024,512]{1,0:T(8,128)} fusion(f32[512,512]{1,0:T(8,128)S(1)} %bitcast.275, s32[1024]{0:T(1024)S(1)} %copy-done.29), kind=kCustom, calls=%fused_computation.6.clone | custom fusion | bytes 4198400 | tf_op jit(solution)/shard_map/jit(_take)/gather | solution.py:41
  378.3 4.9 %gather_fusion.8 = f32[1024,512]{1,0:T(8,128)} fusion(f32[512,512]{1,0:T(8,128)S(1)} %bitcast.276, s32[1024]{0:T(1024)S(1)} %copy-done.28), kind=kCustom, calls=%fused_computation.7.clone | custom fusion | bytes 4198400 | tf_op jit(solution)/shard_map/jit(_take)/gather | solution.py:41
  383.2 4.9 %gather_fusion.5 = f32[1024,512]{1,0:T(8,128)} fusion(f32[512,512]{1,0:T(8,128)S(1)} %bitcast.277, s32[1024]{0:T(1024)S(1)} %copy-done.27), kind=kCustom, calls=%fused_computation.4.clone | custom fusion | bytes 4198400 | tf_op jit(solution)/shard_map/jit(_take)/gather | solution.py:41
  388.2 9.5 %select_reduce_fusion.40 = (f32[1024]{0:T(1024)S(1)}, f32[1024]{0:T(1024)S(1)}, f32[1024]{0:T(1024)S(1)}, f32[1024]{0:T(1024)S(1)}, f32[1024]{0:T(1024)S(1)}, /*...) fusion(f32[1024,512]{1,0:T(8,128)} %gather_fusion.6, ...), kind=kLoop, calls=%fused_computation.230 | loop fusion | flops 20955136 | bytes 8474624 | tf_op jit(solution)/shard_map/reduce_sum | solution.py:42
  398.8 13.8 %while.50 = (s32[]{:T(128)}, f32[2,5,512]{2,1,0:T(8,128)S(1)}, s32[2,512]{1,0:T(2,128)S(1)}, f32[2,2,512]{2,1,0:T(2,128)S(1)}, s32[2,512]{1,0:T(2,128)S(1)}, /*i...) while((s32[]{:T(128)}, f32[2,5,512]{2,1,0:T(8,128)S(1)}, s32[2,512]{1,0:T(2,128)S(1)}, ...), condition=%wide.region_37.39_spmd, body=%wide.region_36.38_spmd.sunk | while | flops 674105344 | bytes 8749185 | solution.py:199
  412.6 4.9 %gather_fusion.10 = f32[1024,512]{1,0:T(8,128)} fusion(f32[512,512]{1,0:T(8,128)S(1)} %bitcast.270, s32[1024]{0:T(1024)S(1)} %get-tuple-element.787), kind=kCustom, calls=%fused_computation.9.clone | custom fusion | bytes 4198400 | tf_op jit(solution)/shard_map/jit(_take)/gather | solution.py:41
  417.5 4.9 %gather_fusion.11 = f32[1024,512]{1,0:T(8,128)} fusion(f32[512,512]{1,0:T(8,128)S(1)} %bitcast.271, s32[1024]{0:T(1024)S(1)} %get-tuple-element.786), kind=kCustom, calls=%fused_computation.10.clone | custom fusion | bytes 4198400 | tf_op jit(solution)/shard_map/jit(_take)/gather | solution.py:41
  422.4 4.9 %gather_fusion.12 = f32[1024,512]{1,0:T(8,128)} fusion(f32[512,512]{1,0:T(8,128)S(1)} %bitcast.272, s32[1024]{0:T(1024)S(1)} %get-tuple-element.785), kind=kCustom, calls=%fused_computation.11.clone | custom fusion | bytes 4198400 | tf_op jit(solution)/shard_map/jit(_take)/gather | solution.py:41
  427.4 4.9 %gather_fusion.9 = f32[1024,512]{1,0:T(8,128)} fusion(f32[512,512]{1,0:T(8,128)S(1)} %bitcast.273, s32[1024]{0:T(1024)S(1)} %copy-done.26), kind=kCustom, calls=%fused_computation.8.clone | custom fusion | bytes 4198400 | tf_op jit(solution)/shard_map/jit(_take)/gather | solution.py:41
  432.4 9.6 %select_reduce_fusion.24 = (f32[1024]{0:T(1024)S(1)}, f32[1024]{0:T(1024)S(1)}, f32[1024]{0:T(1024)S(1)}, f32[1024]{0:T(1024)S(1)}, f32[1024]{0:T(1024)S(1)}, /*...) fusion(f32[1024,512]{1,0:T(8,128)} %gather_fusion.10, ...), kind=kLoop, calls=%fused_computation.210 | loop fusion | flops 20955136 | bytes 8474624 | tf_op jit(solution)/shard_map/reduce_sum | solution.py:42
  444.4 12.7 %while.51 = (s32[]{:T(128)}, f32[2,5,512]{2,1,0:T(8,128)S(1)}, s32[2,512]{1,0:T(2,128)}, f32[2,2,512]{2,1,0:T(2,128)S(1)}, s32[2,512]{1,0:T(2,128)}, /*index=5*/...) while((s32[]{:T(128)}, f32[2,5,512]{2,1,0:T(8,128)S(1)}, s32[2,512]{1,0:T(2,128)}, ...), condition=%wide.region_55.57_spmd, body=%wide.region_54.56_spmd.sunk | while | flops 674105344 | bytes 8749185 | solution.py:199
  460.7 4.9 %gather_fusion.15 = f32[1024,512]{1,0:T(8,128)} fusion(f32[512,512]{1,0:T(8,128)S(1)} %bitcast.267, s32[1024]{0:T(1024)S(1)} %copy-done.20), kind=kCustom, calls=%fused_computation.14.clone | custom fusion | bytes 4198400 | tf_op jit(solution)/shard_map/jit(_take)/gather | solution.py:41
  465.6 4.9 %gather_fusion.16 = f32[1024,512]{1,0:T(8,128)} fusion(f32[512,512]{1,0:T(8,128)S(1)} %bitcast.268, s32[1024]{0:T(1024)S(1)} %copy-done.19), kind=kCustom, calls=%fused_computation.15.clone | custom fusion | bytes 4198400 | tf_op jit(solution)/shard_map/jit(_take)/gather | solution.py:41
  470.7 4.9 %gather_fusion.13 = f32[1024,512]{1,0:T(8,128)} fusion(f32[512,512]{1,0:T(8,128)S(1)} %bitcast.269, s32[1024]{0:T(1024)S(1)} %copy-done.18), kind=kCustom, calls=%fused_computation.12.clone | custom fusion | bytes 4198400 | tf_op jit(solution)/shard_map/jit(_take)/gather | solution.py:41
  476.0 9.2 %select_reduce_fusion.8 = (f32[1024]{0:T(1024)S(1)}, f32[1024]{0:T(1024)S(1)}, f32[1024]{0:T(1024)S(1)}, f32[1024]{0:T(1024)S(1)}, f32[1024]{0:T(1024)S(1)}, /*i...) fusion(f32[1024,512]{1,0:T(8,128)S(1)} %gather_fusion.14, ...), kind=kLoop, calls=%fused_computation.190 | loop fusion | flops 20955136 | bytes 8474624 | tf_op jit(solution)/shard_map/reduce_sum | solution.py:42
  (336 shorter events, 180.9 us)
Async XLA Ops:
  0.6 24.1 %copy-start = (bf16[1,1024,256]{2,1,0:T(8,128)(2,1)S(1)}, bf16[1,1024,256]{2,1,0:T(8,128)(2,1)}, u32[]{:S(2)}) copy-start(bf16[1,1024,256]{2,1,0:T(8,128)(2,1)} %param.23) | copy-start | bytes 1572868
  2.2 21.1 %all-to-all-start = ((s32[128,1,16]{2,1,0:T(1,128)}), s32[128,1,16]{2,1,0:T(1,128)S(1)}, u32[]{:S(2)}, u32[]{:S(2)}) async-start(s32[128,1,16]{2,1,0:T(1,128)} %bitcast.38), calls=%async_computation | async-start | bytes 131072 | tf_op jit(solution)/shard_map/all_to_all | solution.py:147
  32.3 11.3 %copy-start.5 = (f32[2,1024]{1,0:T(2,128)S(1)}, f32[2,1024]{1,0:T(2,128)}, u32[]{:S(2)}) copy-start(f32[2,1024]{1,0:T(2,128)} %param.29) | copy-start | bytes 24580
  32.3 11.3 %copy-start.11 = (s32[4,1024]{1,0:T(4,128)S(1)}, s32[4,1024]{1,0:T(4,128)}, u32[]{:S(2)}) copy-start(s32[4,1024]{1,0:T(4,128)} %param.26) | copy-start | bytes 49156
  32.3 29.9 %copy-start.12 = (f32[16,512]{1,0:T(8,128)S(1)}, f32[16,512]{1,0:T(8,128)}, u32[]{:S(2)}) copy-start(f32[16,512]{1,0:T(8,128)} %param.22) | copy-start | bytes 98308
  33.5 28.6 %all-to-all-start.1 = ((bf16[128,16,256]{2,1,0:T(8,128)(2,1)}), bf16[128,16,256]{2,1,0:T(8,128)(2,1)S(1)}, u32[]{:S(2)}, u32[]{:S(2)}) async-start(bf16[128,16,256]{2,1,0:T(8,128)(2,1)} %broadcast_select_fusion), calls=%async_computation.1 | async-start | bytes 2097152 | tf_op jit(solution)/shard_map/all_to_all | solution.py:157
  64.7 243.1 %all-to-all-start.2 = ((f32[128,16,512]{2,1,0:T(8,128)}), f32[128,16,512]{2,1,0:T(8,128)}, u32[]{:S(2)}, u32[]{:S(2)}) async-start(f32[128,16,512]{2,1,0:T(8,128)} %stack.128), calls=%async_computation.2 | async-start | bytes 8388608 | tf_op jit(solution)/shard_map/all_to_all | solution.py:166
  124.1 6.6 %copy-start.2 = (f32[32,16,256]{2,1,0:T(8,128)S(1)}, f32[32,16,256]{2,1,0:T(8,128)}, u32[]{:S(2)}) copy-start(f32[32,16,256]{2,1,0:T(8,128)} %get-tuple-element.623) | copy-start | bytes 1572868
  243.9 34.3 %copy-start.3 = (bf16[512,5,16,16]{0,3,2,1:T(8,128)(2,1)S(1)}, bf16[512,5,16,16]{0,3,2,1:T(8,128)(2,1)}, u32[]{:S(2)}) copy-start(bf16[512,5,16,16]{0,3,2,1:T(8,128)(2,1)} %constant_dynamic-update-slice_fusion.14) | copy-start | bytes 3932164
  331.1 6.6 %copy-start.32 = (s32[1024]{0:T(1024)S(1)}, s32[1024]{0:T(1024)}, u32[]{:S(2)}) copy-start(s32[1024]{0:T(1024)} %get-tuple-element.779) | copy-start | bytes 12292
  331.1 6.6 %copy-start.33 = (s32[1024]{0:T(1024)S(1)}, s32[1024]{0:T(1024)}, u32[]{:S(2)}) copy-start(s32[1024]{0:T(1024)} %get-tuple-element.780) | copy-start | bytes 12292
  331.1 6.6 %copy-start.61 = (pred[1024]{0:T(1024)(128)(4,1)S(1)}, pred[1024]{0:T(1024)(128)(4,1)}, u32[]{:S(2)}) copy-start(pred[1024]{0:T(1024)(128)(4,1)} %get-tuple-element.551) | copy-start | bytes 3076
  331.1 6.6 %copy-start.62 = (pred[1024]{0:T(1024)(128)(4,1)S(1)}, pred[1024]{0:T(1024)(128)(4,1)}, u32[]{:S(2)}) copy-start(pred[1024]{0:T(1024)(128)(4,1)} %get-tuple-element.774) | copy-start | bytes 3076
  331.1 6.6 %copy-start.63 = (pred[1024]{0:T(1024)(128)(4,1)S(1)}, pred[1024]{0:T(1024)(128)(4,1)}, u32[]{:S(2)}) copy-start(pred[1024]{0:T(1024)(128)(4,1)} %get-tuple-element.775) | copy-start | bytes 3076
  331.1 6.6 %copy-start.64 = (pred[1024]{0:T(1024)(128)(4,1)S(1)}, pred[1024]{0:T(1024)(128)(4,1)}, u32[]{:S(2)}) copy-start(pred[1024]{0:T(1024)(128)(4,1)} %get-tuple-element.776) | copy-start | bytes 3076
  337.7 10.0 %copy-start.38 = (f32[1,1024]{1,0:T(1,128)S(1)}, f32[1,1024]{1,0:T(1,128)}, u32[]{:S(2)}) copy-start(f32[1,1024]{1,0:T(1,128)} %get-tuple-element.548) | copy-start | bytes 12292
  337.7 10.0 %copy-start.39 = (f32[1,1024]{1,0:T(1,128)S(1)}, f32[1,1024]{1,0:T(1,128)}, u32[]{:S(2)}) copy-start(f32[1,1024]{1,0:T(1,128)} %get-tuple-element.714) | copy-start | bytes 12292
  337.7 10.0 %copy-start.40 = (f32[1,1024]{1,0:T(1,128)S(1)}, f32[1,1024]{1,0:T(1,128)}, u32[]{:S(2)}) copy-start(f32[1,1024]{1,0:T(1,128)} %get-tuple-element.715) | copy-start | bytes 12292
  337.7 10.0 %copy-start.41 = (f32[1,1024]{1,0:T(1,128)S(1)}, f32[1,1024]{1,0:T(1,128)}, u32[]{:S(2)}) copy-start(f32[1,1024]{1,0:T(1,128)} %get-tuple-element.716) | copy-start | bytes 12292
  337.7 10.0 %copy-start.45 = (f32[5]{0:T(128)S(1)}, f32[5]{0:T(128)}, u32[]{:S(2)}) copy-start(f32[5]{0:T(128)} %constant.668.clone) | copy-start | bytes 64
  337.8 10.7 %copy-start.34 = (s32[4,1024]{1,0:T(4,128)S(1)}, s32[4,1024]{1,0:T(4,128)}, u32[]{:S(2)}) copy-start(s32[4,1024]{1,0:T(4,128)} %param.28) | copy-start | bytes 49156
  349.2 19.3 %copy-start.30 = (s32[1024]{0:T(1024)S(1)}, s32[1024]{0:T(1024)}, u32[]{:S(2)}) copy-start(s32[1024]{0:T(1024)} %get-tuple-element.760) | copy-start | bytes 12292
  388.2 9.8 %copy-start.43 = (f32[1,1024]{1,0:T(1,128)S(1)}, f32[1,1024]{1,0:T(1,128)}, u32[]{:S(2)}) copy-start(f32[1,1024]{1,0:T(1,128)} %get-tuple-element.543) | copy-start | bytes 12292
  388.2 9.8 %copy-start.46 = (f32[5]{0:T(128)S(1)}, f32[5]{0:T(128)}, u32[]{:S(2)}) copy-start(f32[5]{0:T(128)} %constant.668.clone) | copy-start | bytes 64
  432.4 9.9 %copy-start.44 = (f32[1,1024]{1,0:T(1,128)S(1)}, f32[1,1024]{1,0:T(1,128)}, u32[]{:S(2)}) copy-start(f32[1,1024]{1,0:T(1,128)} %get-tuple-element.538) | copy-start | bytes 12292
  432.4 9.9 %copy-start.47 = (f32[5]{0:T(128)S(1)}, f32[5]{0:T(128)}, u32[]{:S(2)}) copy-start(f32[5]{0:T(128)} %constant.668.clone) | copy-start | bytes 64
  432.4 12.0 %copy-start.4 = (bf16[512,1280]{1,0:T(8,128)(2,1)S(1)}, bf16[512,1280]{1,0:T(8,128)(2,1)}, u32[]{:S(2)}) copy-start(bf16[512,1280]{1,0:T(8,128)(2,1)} %copy.85) | copy-start | bytes 3932164
  444.4 12.8 %copy-start.21 = (s32[1024]{0:T(1024)S(1)}, s32[1024]{0:T(1024)}, u32[]{:S(2)}) copy-start(s32[1024]{0:T(1024)} %get-tuple-element.738) | copy-start | bytes 12292
  475.9 9.5 %copy-start.42 = (f32[1,1024]{1,0:T(1,128)S(1)}, f32[1,1024]{1,0:T(1,128)}, u32[]{:S(2)}) copy-start(f32[1,1024]{1,0:T(1,128)} %get-tuple-element.531) | copy-start | bytes 12292
  475.9 9.5 %copy-start.48 = (f32[5]{0:T(128)S(1)}, f32[5]{0:T(128)}, u32[]{:S(2)}) copy-start(f32[5]{0:T(128)} %constant.668.clone) | copy-start | bytes 64
  475.9 9.6 %copy-start.13 = (f32[2,1024]{1,0:T(2,128)S(1)}, f32[2,1024]{1,0:T(2,128)}, u32[]{:S(2)}) copy-start(f32[2,1024]{1,0:T(2,128)} %get-tuple-element.537) | copy-start | bytes 24580
  476.0 10.9 %copy-start.1 = (bf16[1,1024,256]{2,1,0:T(8,128)(2,1)S(1)}, bf16[1,1024,256]{2,1,0:T(8,128)(2,1)}, u32[]{:S(2)}) copy-start(bf16[1,1024,256]{2,1,0:T(8,128)(2,1)} %param.23) | copy-start | bytes 1572868
  (36 other events, 181.9 us)
